TPU v7x, 32 devices: a whole 2x2x4 slice. The times are simulated.
32 devices in a mesh: groups: 2 (over x), row: 8 (over z, y), col: 2 (over core).
Axes of the slice: x: 2, y: 2, z: 4, core: 2. Of those that a mesh axis runs over, the one named last changes fastest.
Arguments:
- queries: bfloat16 [512, 32, 128], P(('groups', 'row', 'col')), parts along dimension 0, may hold values from -4 to 4
- clauses: bfloat16 [512, 32, 128], P(('groups', 'row', 'col')), parts along dimension 0, may hold values from -4 to 4
- pattern: int32 [32, 16], P('groups'), parts along dimension 0, may hold values from 0 to 1, as said below
- positive: int32 [512], P(('groups', 'row', 'col')), parts along dimension 0, may hold values from 0 to 255, as said below
Outputs:
- per_query: float32 [512], P(('groups', 'row', 'col')), parts along dimension 0
- grad_queries: float32 [512, 32, 128], P(('groups', 'row', 'col')), parts along dimension 0
- grad_clauses: float32 [512, 32, 128], P(('groups', 'row', 'col')), parts along dimension 0
There are 2 independent parts, one for each index of `groups`. A program takes and returns all parts, laid end to end along the dimension named above; each array names one. Nothing has to cross between parts.
Inputs may be any that keep to these rules, and one draw needn't show every extreme that they name: Block a holds rows a * 16 to a * 16 + 15; pattern[a, a] = 1 for every block a. positive is a permutation of the rows, and positive[i] lies in the same block of 16 rows as i.
All inputs are finite; a program needn't handle non-finite values.
Results may differ from a plain program's by a relative error of at most 0.0027.
Values may be sent and summed in bfloat16 or wider, within the bound.
A program may use at most 64 MiB of HBM per device.

v0:
```python
import functools
import math

import jax
import jax.numpy as jnp
from jax import lax
from jax.experimental import pallas as pl
from jax.experimental.pallas import tpu as pltpu
from jax.sharding import PartitionSpec as P

SHARPNESS = 3.0
FLOOR_VALUE = -1e30
EXP2_SCALE = SHARPNESS * math.log2(math.e)
LN2 = math.log(2.0)
AXES = ("row", "col")
F32 = jnp.float32
BF16 = jnp.bfloat16


def dot(a, b, dims):
    return lax.dot_general(a, b, (dims, ((), ())), preferred_element_type=F32)


def split3(x):
    hi = x.astype(BF16)
    rest = x - hi.astype(F32)
    mid = rest.astype(BF16)
    return hi, mid, (rest - mid.astype(F32)).astype(BF16)


def exact_dot(parts, other, dims):
    hi, mid, low = (dot(part, other, dims) for part in parts)
    return hi + (mid + low)


def token_indicator(count, length):
    width = count * length
    item = lax.broadcasted_iota(jnp.int32, (count, width), 0)
    token = lax.broadcasted_iota(jnp.int32, (count, width), 1)
    start = item * length
    return jnp.where((token >= start) & (token < start + length), 1.0, 0.0).astype(BF16)


def position():
    return lax.axis_index("row") * lax.axis_size("col") + lax.axis_index("col")


def score_kernel(dims, pattern_ref, queries_ref, clauses_ref, mask_ref, out_ref, lse_ref):
    block, length, chunk = dims
    place = position()
    tokens = block * length
    blocks = clauses_ref.shape[0] // tokens
    lse_ref[...] = jnp.zeros_like(lse_ref)

    @pl.loop(0, blocks)
    def _(b):
        @pl.when(pattern_ref[place, b] > 0)
        def _():
            for c in range(block // chunk):
                start = pl.multiple_of(b * tokens + c * chunk * length, chunk * length)
                logits = dot(clauses_ref[pl.ds(start, chunk * length), :], queries_ref[...], ((1,), (1,)))
                logits = logits.reshape(chunk, length, tokens)
                top = jnp.max(logits, axis=1)
                total = jnp.sum(jnp.exp2((logits - top[:, None, :]) * EXP2_SCALE), axis=1)
                lse_ref[pl.ds(pl.multiple_of(b * block + c * chunk, chunk), chunk), :] = (
                    top * SHARPNESS + jnp.log(total)
                )

    indicator = token_indicator(block, length)
    hi, mid, low = split3(lse_ref[...])
    sums = dot(indicator, hi, ((1,), (1,))) + (
        dot(indicator, mid, ((1,), (1,))) + dot(indicator, low, ((1,), (1,)))
    )
    out_ref[...] = jnp.where(mask_ref[...] > 0, sums / SHARPNESS, FLOOR_VALUE)


def softmax_weights(logits, factor, chunk, length):
    logits = logits.reshape(chunk, length, logits.shape[1])
    top = jnp.max(logits, axis=1, keepdims=True)
    raised = jnp.exp2((logits - top) * EXP2_SCALE)
    total = jnp.sum(raised, axis=1)
    weights = raised * (factor / total)[:, None, :]
    return weights.reshape(chunk * length, logits.shape[2]).astype(BF16)


def grad_kernel(
    dims, pattern_ref, queries_ref, clauses_ref, own_q_ref, own_c_ref, scores_ref, positive_ref,
    per_query_ref, grad_q_ref, grad_c_ref,
    row_factor_ref, col_factor_ref, weights_ref, grad_qt_ref,
):
    block, length, chunk = dims
    place = position()
    tokens = block * length
    blocks = clauses_ref.shape[0] // tokens
    own = pl.multiple_of(place * block, block)
    indicator = token_indicator(block, length)
    total_rows = scores_ref.shape[0]

    scores = scores_ref[...]
    row_top = jnp.max(scores, axis=1, keepdims=True)
    row_lse = row_top + jnp.log(jnp.sum(jnp.exp(scores - row_top), axis=1, keepdims=True))
    col_top = jnp.max(scores, axis=0, keepdims=True)
    col_lse = col_top + jnp.log(jnp.sum(jnp.exp(scores - col_top), axis=0, keepdims=True))

    mine = scores_ref[pl.ds(own, block), :]
    mine_top = jnp.max(mine, axis=1, keepdims=True)
    mine_lse = mine_top + jnp.log(jnp.sum(jnp.exp(mine - mine_top), axis=1, keepdims=True))
    positive = positive_ref[...]
    matches = positive == lax.broadcasted_iota(jnp.int32, (block, total_rows), 1)
    positive_score = jnp.sum(jnp.where(matches, mine, 0.0), axis=1, keepdims=True)
    positive_col = jnp.sum(jnp.where(matches, col_lse, 0.0), axis=1, keepdims=True)
    per_query_ref[...] = 0.5 * (mine_lse - positive_score) + 0.5 * (positive_col - positive_score)

    row_factor = 0.5 * (jnp.exp(mine - mine_lse) + jnp.exp(mine - col_lse)) - jnp.where(matches, 1.0, 0.0)
    row_factor_ref[...] = exact_dot(split3(row_factor), indicator, ((0,), (0,)))

    factor = 0.5 * (jnp.exp(scores - row_lse) + jnp.exp(scores - col_lse))
    col_factor_ref[...] = pltpu.roll(factor, total_rows - own, 1)[:, :128]
    local = positive - own == lax.broadcasted_iota(jnp.int32, (block, 128), 1)
    col_factor_ref[pl.ds(own, block), :] = col_factor_ref[pl.ds(own, block), :] - jnp.where(local, 1.0, 0.0)

    grad_qt_ref[...] = jnp.zeros_like(grad_qt_ref)
    grad_c_ref[...] = jnp.zeros_like(grad_c_ref)

    @pl.loop(0, blocks)
    def _(b):
        base = pl.multiple_of(b * tokens, tokens)

        @pl.when(pattern_ref[place, b] > 0)
        def _():
            for c in range(block // chunk):
                start = pl.multiple_of(base + c * chunk * length, chunk * length)
                logits = dot(clauses_ref[pl.ds(start, chunk * length), :], own_q_ref[...], ((1,), (1,)))
                factor_tile = row_factor_ref[pl.ds(pl.multiple_of(b * block + c * chunk, chunk), chunk), :]
                weights_ref[pl.ds(c * chunk * length, chunk * length), :] = softmax_weights(
                    logits, factor_tile, chunk, length
                )
            grad_qt_ref[...] += dot(clauses_ref[pl.ds(base, tokens), :], weights_ref[...], ((0,), (0,)))

        @pl.when(pattern_ref[b, place] > 0)
        def _():
            block_factor = col_factor_ref[pl.ds(pl.multiple_of(b * block, block), block), :][:, :block]
            spread = exact_dot(split3(block_factor), indicator, ((0,), (0,)))
            query_tile = queries_ref[pl.ds(base, tokens), :]
            for c in range(block // chunk):
                logits = dot(own_c_ref[pl.ds(c * chunk * length, chunk * length), :], query_tile, ((1,), (1,)))
                weights_ref[pl.ds(c * chunk * length, chunk * length), :] = softmax_weights(
                    logits, spread[c * chunk : (c + 1) * chunk], chunk, length
                )
            grad_c_ref[...] += dot(weights_ref[...], query_tile, ((1,), (0,)))

    grad_q_ref[...] = grad_qt_ref[...].T


def shards(queries, clauses, pattern, positive):
    block, length, width = queries.shape
    blocks = pattern.shape[0]
    tokens = block * length
    total_rows = blocks * block
    dims = (block, length, 8)
    own_q = queries.reshape(tokens, width)
    own_c = clauses.reshape(tokens, width)
    all_c = lax.all_gather(own_c, AXES, axis=0, tiled=True)
    all_q = lax.all_gather(own_q, AXES, axis=0, tiled=True)
    mask = jnp.repeat(lax.dynamic_slice_in_dim(pattern, lax.axis_index(AXES), 1, 0), block, axis=1)
    smem = pl.BlockSpec(memory_space=pltpu.SMEM)
    vmem = pl.BlockSpec(memory_space=pltpu.VMEM)
    params = pltpu.CompilerParams(vmem_limit_bytes=40 * 1024 * 1024)
    scores = pl.pallas_call(
        functools.partial(score_kernel, dims),
        out_shape=jax.ShapeDtypeStruct((block, total_rows), F32),
        in_specs=[smem, vmem, vmem, vmem],
        out_specs=vmem,
        scratch_shapes=[pltpu.VMEM((total_rows, tokens), F32)],
        compiler_params=params,
        cost_estimate=pl.CostEstimate(flops=2 * 10**9, bytes_accessed=4 * 10**6, transcendentals=2 * 10**6),
        name="scores",
    )(pattern, own_q, all_c, mask)
    all_scores = lax.all_gather(scores, AXES, axis=0, tiled=True)
    per_query, grad_q, grad_c = pl.pallas_call(
        functools.partial(grad_kernel, dims),
        out_shape=(
            jax.ShapeDtypeStruct((block, 1), F32),
            jax.ShapeDtypeStruct((tokens, width), F32),
            jax.ShapeDtypeStruct((tokens, width), F32),
        ),
        in_specs=[smem] + [vmem] * 6,
        out_specs=(vmem, vmem, vmem),
        scratch_shapes=[
            pltpu.VMEM((total_rows, tokens), F32),
            pltpu.VMEM((total_rows, 128), F32),
            pltpu.VMEM((tokens, tokens), BF16),
            pltpu.VMEM((width, tokens), F32),
        ],
        compiler_params=params,
        name="grads",
    )(pattern, all_q, all_c, own_q, own_c, all_scores, positive[:, None])
    return (
        per_query.reshape(block),
        grad_q.reshape(queries.shape),
        grad_c.reshape(clauses.shape),
    )


def solution(mesh):
    rows = P(("groups", "row", "col"), None, None)
    ids = P(("groups", "row", "col"))
    return jax.shard_map(
        shards,
        mesh=mesh,
        in_specs=(rows, rows, P("groups", None), ids),
        out_specs=(ids, rows, rows),
        check_vma=False,
    )
```

profile of v0, /device:TPU:0, one launch (start us, length us, event | category | flops | bytes accessed | tf_op | source)
XLA Modules:
  0.0 118.0 jit_solution(15939862997995943326)
XLA Ops:
  7.2 0.0 all-gather.5.cloned.1.call-start
  7.2 0.7 all-gather.5.cloned.1.call-update
  7.9 0.0 all-gather.3.cloned.1.call-start
  7.9 0.7 all-gather.3.cloned.1.call-update
  8.7 0.7 dynamic-slice_bitcast_fusion
  9.3 0.1 broadcast_in_dim.8
  9.4 0.1 broadcast_in_dim.9.mask_ref
  9.5 0.7 copy.8.positive_ref
  10.2 44.0 %all-gather.5.cloned.1.call-done.clauses_ref = bf16[8192,128]{1,0:T(8,128)(2,1)} async-done(((bf16[512,128]{1,0:T(8,128)(2,1)}), bf16[8192,128]{1,0:T(8,128)(2,1)}) %all-gather.5.cloned.1.call-update) | async-done | bytes 2097168 | tf_op jit(solution)/shard_map/all_gather | solution.py:163
  54.3 0.0 copy-start
  54.3 1.6 %copy-done = bf16[8192,128]{1,0:T(8,128)(2,1)S(1)} copy-done((bf16[8192,128]{1,0:T(8,128)(2,1)S(1)}, bf16[8192,128]{1,0:T(8,128)(2,1)}, u32[]{:S(2)}) %copy-start) | copy-done | bytes 2097176
  55.9 0.9 copy-done.4
  56.8 0.7 copy-done.6
  57.5 5.1 %scores.1 = f32[16,256]{1,0:T(8,128)S(1)} custom-call(s32[16,16]{1,0:T(8,128)S(1)} %copy-done.6, bf16[512,128]{1,0:T(8,128)(2,1)S(1)} %bitcast.10, bf16[8192,128]{1,0:T(8,128)(2,1)S(1)} %copy-done, s32[1,256]{1,0:T(1,128)S(1)} %broadcast_in_dim.9.mask_ref), custom_call_target="tpu_custom_call" | custom-call | flops 2000000000 | bytes 4000000 | tf_op jit(solution)/shard_map/scores/pallas_call | solution.py:169
  62.6 18.5 %all_gather.11.scores_ref = f32[256,256]{1,0:T(8,128)S(1)} all-gather(f32[16,256]{1,0:T(8,128)S(1)} %scores.1), channel_id=1, replica_groups=mesh['groups'=2,'row'=8,'col'=2] {'row','col'}, dimensions={0}, use_global_device_ids=true | all-gather | bytes 278528 | tf_op jit(solution)/shard_map/all_gather | solution.py:179
  81.1 15.8 %all-gather.3.cloned.1.call-done.queries_ref = bf16[8192,128]{1,0:T(8,128)(2,1)} async-done(((bf16[512,128]{1,0:T(8,128)(2,1)}), bf16[8192,128]{1,0:T(8,128)(2,1)}) %all-gather.3.cloned.1.call-update) | async-done | bytes 2097168 | tf_op jit(solution)/shard_map/all_gather | solution.py:164
  96.9 0.0 copy-done.1
  96.9 0.0 copy-done.3
  96.9 0.0 copy-done.5
  96.9 0.0 copy-done.7
  96.9 0.0 copy-start.2
  96.9 1.6 %copy-done.2 = bf16[8192,128]{1,0:T(8,128)(2,1)S(1)} copy-done((bf16[8192,128]{1,0:T(8,128)(2,1)S(1)}, bf16[8192,128]{1,0:T(8,128)(2,1)}, u32[]{:S(2)}) %copy-start.2) | copy-done | bytes 2097176
  98.5 12.1 %grads.1 = (f32[16,1]{1,0:T(8,128)S(1)}, f32[512,128]{1,0:T(8,128)}, f32[512,128]{1,0:T(8,128)}) custom-call(s32[16,16]{1,0:T(8,128)S(1)} %copy-done.7, bf16[8192,128]{1,0:T(8,128)(2,1)S(1)} %copy-done.2, bf16[8192,128]{1,0:T(8,128)(2,1)S(1)} %copy-done.1, bf16[512,128]{1,0:T(8,128)(2,1)S(1)} %bitcast.11, bf16[512,128]{1,0:T(8,128)(2,1)S(1)} %bitcast.8, ...), custom_call_target="tpu_custom_call" | custom-call | tf_op jit(solution)/shard_map/grads/pallas_call | solution.py:180
  110.6 0.6 reduce
  (6 shorter events, 0.0 us)
Async XLA Ops:
  7.2 47.1 %all-gather.5.cloned.1.call-start = ((), (), s32[]{:S(2)}) async-start(), calls=%async_computation.1 | async-start | bytes 2228224 | tf_op jit(solution)/shard_map/all_gather | solution.py:163
  7.9 89.0 %all-gather.3.cloned.1.call-start = ((), (), s32[]{:S(2)}) async-start(), calls=%async_computation | async-start | bytes 2228224 | tf_op jit(solution)/shard_map/all_gather | solution.py:164
  54.3 1.6 %copy-start = (bf16[8192,128]{1,0:T(8,128)(2,1)S(1)}, bf16[8192,128]{1,0:T(8,128)(2,1)}, u32[]{:S(2)}) copy-start(bf16[8192,128]{1,0:T(8,128)(2,1)} %all-gather.5.cloned.1.call-done.clauses_ref) | copy-start | bytes 6291460
  55.9 0.9 copy-start.4
  56.8 0.7 copy-start.6
  57.5 39.4 %copy-start.1 = (bf16[8192,128]{1,0:T(8,128)(2,1)S(1)}, bf16[8192,128]{1,0:T(8,128)(2,1)}, u32[]{:S(2)}) copy-start(bf16[8192,128]{1,0:T(8,128)(2,1)} %all-gather.5.cloned.1.call-done.clauses_ref) | copy-start | bytes 6291460
  57.5 39.4 %copy-start.3 = (bf16[16,32,128]{2,1,0:T(8,128)(2,1)S(1)}, bf16[16,32,128]{2,1,0:T(8,128)(2,1)}, u32[]{:S(2)}) copy-start(bf16[16,32,128]{2,1,0:T(8,128)(2,1)} %param.5) | copy-start | bytes 393220
  57.5 39.4 %copy-start.5 = (bf16[16,32,128]{2,1,0:T(8,128)(2,1)S(1)}, bf16[16,32,128]{2,1,0:T(8,128)(2,1)}, u32[]{:S(2)}) copy-start(bf16[16,32,128]{2,1,0:T(8,128)(2,1)} %param.4) | copy-start | bytes 393220
  57.5 39.4 %copy-start.7 = (s32[16,16]{1,0:T(8,128)S(1)}, s32[16,16]{1,0:T(8,128)}, u32[]{:S(2)}) copy-start(s32[16,16]{1,0:T(8,128)} %pattern_ref.3) | copy-start | bytes 3076
  96.9 1.6 %copy-start.2 = (bf16[8192,128]{1,0:T(8,128)(2,1)S(1)}, bf16[8192,128]{1,0:T(8,128)(2,1)}, u32[]{:S(2)}) copy-start(bf16[8192,128]{1,0:T(8,128)(2,1)} %all-gather.3.cloned.1.call-done.queries_ref) | copy-start | bytes 6291460
Sparse Core Ops, SparseCore 0:
  10.2 44.0 all-gather.4
  56.5 40.3 all-gather.2
where the time goes:
time: 119 us; the launch traced here: 118 us
  waiting for transfers between devices  61.2 us (51%)
  blocking collectives  18.5 us (16%)
  Pallas kernels  17.2 us (14%)
  between operations  14.1 us (12%)
  local copies, waits for them, and re-layouts  6.38 us (5%)
    all_gather x1, waiting for transfers between devices, shards(): all_c = lax.all_gather(own_c, AXES, axis=0, tiled=True)  44 us
    all_gather x1, blocking collectives, shards(): all_scores = lax.all_gather(scores, AXES, axis=0, tiled=True)  18.5 us
    all_gather x1, waiting for transfers between devices, shards(): all_q = lax.all_gather(own_q, AXES, axis=0, tiled=True)  15.8 us
    pallas_call x1, Pallas kernels, shards(): pl.pallas_call(functools.partial(grad_kernel, dims), out_shape=(jax.Shape...  12.1 us
    pallas_call x1, Pallas kernels, shards(): pl.pallas_call(functools.partial(score_kernel, dims), out_shape=jax.Shape...  5.1 us
    unnamed x16, local copies, waits for them, and re-layouts  4.79 us
  transfers between devices with their start and end apart: 2, of which 2 were waited for; matrix products, arithmetic and copies ran while one was open for 1% of the time, Pallas kernels for 4%

commit v1 on v0

--- a/solution.py
+++ b/solution.py
@@ -43,6 +43,117 @@
 
 def position():
     return lax.axis_index("row") * lax.axis_size("col") + lax.axis_index("col")
+
+
+def ring_place(row, count):
+    if count != 8:
+        return row
+    side = row % 2
+    return (row // 2) * (1 - side) + (7 - row // 2) * side
+
+
+def ring_row(place, count):
+    if count != 8:
+        return place
+    side = place // 4
+    return 2 * (place * (1 - side) + (7 - place) * side) + side
+
+
+def gather_kernel(count, rows, *refs):
+    arrays = len(rows)
+    own, full = refs[:arrays], refs[arrays : 2 * arrays]
+    hop_send, hop_recv, push_send, push_recv = refs[2 * arrays :]
+    row, core = lax.axis_index("row"), lax.axis_index("col")
+    sibling = {"col": 1 - core}
+    place = ring_place(row, count)
+    ahead = {"row": ring_row((place + 1) % count, count)}
+    behind = {"row": ring_row((place + count - 1) % count, count)}
+    last = count // 2
+
+    def block_start(a, source):
+        return pl.multiple_of((source * 2 + core) * rows[a], rows[a])
+
+    def piece(a, way, step):
+        if step < last:
+            return 0, rows[a]
+        return way * (rows[a] // 2), rows[a] // 2
+
+    def hop(a, way, step):
+        shift = step - 1
+        origin = (place + count - shift) % count if way == 0 else (place + shift) % count
+        offset, size = piece(a, way, step)
+        start = block_start(a, ring_row(origin, count)) + offset
+        target = full[a].at[pl.ds(start, size), :]
+        return pltpu.make_async_remote_copy(
+            src_ref=own[a].at[pl.ds(offset, size), :] if step == 1 else target,
+            dst_ref=target,
+            send_sem=hop_send.at[a, way, step - 1],
+            recv_sem=hop_recv.at[a, way, step - 1],
+            device_id=ahead if way == 0 else behind,
+            device_id_type=pl.DeviceIdType.MESH,
+        )
+
+    def push(a, way, step):
+        offset, size = piece(a, way, step)
+        origin = (place + count - step) % count if way == 0 else (place + step) % count
+        target = full[a].at[pl.ds(block_start(a, ring_row(origin, count)) + offset, size), :]
+        return pltpu.make_async_remote_copy(
+            src_ref=own[a] if step == 0 else target,
+            dst_ref=target,
+            send_sem=push_send.at[a, way, step],
+            recv_sem=push_recv.at[a, way, step],
+            device_id=sibling,
+            device_id_type=pl.DeviceIdType.MESH,
+        )
+
+    barrier = pltpu.get_barrier_semaphore()
+    for peer in (ahead, behind, sibling):
+        pl.semaphore_signal(barrier, inc=1, device_id=peer, device_id_type=pl.DeviceIdType.MESH)
+    pl.semaphore_wait(barrier, 3)
+
+    for a in range(arrays):
+        for way in (0, 1):
+            hop(a, way, 1).start()
+        push(a, 0, 0).start()
+    for a in range(arrays):
+        full[a][pl.ds(block_start(a, row), rows[a]), :] = own[a][...]
+    for step in range(1, last + 1):
+        for a in range(arrays):
+            for way in (0, 1):
+                hop(a, way, step).wait_recv()
+                if step < last:
+                    hop(a, way, step + 1).start()
+                push(a, way, step).start()
+    for a in range(arrays):
+        push(a, 0, 0).wait()
+        for step in range(1, last + 1):
+            for way in (0, 1):
+                hop(a, way, step).wait_send()
+                push(a, way, step).wait()
+
+
+def gathered(blocks, collective_id, name, *arrays):
+    count = lax.axis_size("row")
+    steps = count // 2
+    vmem = pl.BlockSpec(memory_space=pltpu.VMEM)
+    sems = pltpu.SemaphoreType.DMA
+    many = len(arrays)
+    return pl.pallas_call(
+        functools.partial(gather_kernel, count, tuple(a.shape[0] for a in arrays)),
+        out_shape=tuple(jax.ShapeDtypeStruct((blocks * a.shape[0], a.shape[1]), a.dtype) for a in arrays),
+        in_specs=[vmem] * many,
+        out_specs=(vmem,) * many,
+        scratch_shapes=[
+            sems((many, 2, steps)),
+            sems((many, 2, steps)),
+            sems((many, 2, steps + 1)),
+            sems((many, 2, steps + 1)),
+        ],
+        compiler_params=pltpu.CompilerParams(
+            collective_id=collective_id, has_side_effects=True, vmem_limit_bytes=40 * 1024 * 1024
+        ),
+        name=name,
+    )(*arrays)
 
 
 def score_kernel(dims, pattern_ref, queries_ref, clauses_ref, mask_ref, out_ref, lse_ref):
@@ -160,8 +271,7 @@
     dims = (block, length, 8)
     own_q = queries.reshape(tokens, width)
     own_c = clauses.reshape(tokens, width)
-    all_c = lax.all_gather(own_c, AXES, axis=0, tiled=True)
-    all_q = lax.all_gather(own_q, AXES, axis=0, tiled=True)
+    all_c, all_q = gathered(blocks, 0, "gather_tokens", own_c, own_q)
     mask = jnp.repeat(lax.dynamic_slice_in_dim(pattern, lax.axis_index(AXES), 1, 0), block, axis=1)
     smem = pl.BlockSpec(memory_space=pltpu.SMEM)
     vmem = pl.BlockSpec(memory_space=pltpu.VMEM)
@@ -176,7 +286,7 @@
         cost_estimate=pl.CostEstimate(flops=2 * 10**9, bytes_accessed=4 * 10**6, transcendentals=2 * 10**6),
         name="scores",
     )(pattern, own_q, all_c, mask)
-    all_scores = lax.all_gather(scores, AXES, axis=0, tiled=True)
+    (all_scores,) = gathered(blocks, 1, "gather_scores", scores)
     per_query, grad_q, grad_c = pl.pallas_call(
         functools.partial(grad_kernel, dims),
         out_shape=(

time: 119 us -> 64.8 us (0.54)
  the two profiles are of different devices: /device:TPU:0 before, /device:TPU:1 now
where the time goes in v1:
time: 64.8 us; the launch traced here: 65.7 us
  Pallas kernels  60.3 us (93%)
  local copies, waits for them, and re-layouts  4.09 us (6%)
  between operations  0.68 us (1%)
    pallas_call x2, Pallas kernels, gathered(): pl.pallas_call(functools.partial(gather_kernel, count, tuple((a.shape[0]...  42.4 us
    pallas_call x1, Pallas kernels, shards(): pl.pallas_call(functools.partial(grad_kernel, dims), out_shape=(jax.Shape...  12.9 us
    pallas_call x1, Pallas kernels, shards(): pl.pallas_call(functools.partial(score_kernel, dims), out_shape=jax.Shape...  5.1 us
    unnamed x10, local copies, waits for them, and re-layouts  2.51 us

profile of v1, /device:TPU:1, one launch (start us, length us, event | category | flops | bytes accessed | tf_op | source)
XLA Modules:
  0.0 65.7 jit_solution(6715275958552273806)
XLA Ops:
  0.6 0.7 %dynamic-slice_bitcast_fusion = s32[16]{0:T(128)S(1)} fusion(s32[16,16]{1,0:T(8,128)} %pattern_ref.3, s32[]{:T(128)S(6)} %select_n.3), kind=kLoop, calls=%fused_computation | loop fusion | bytes 132 | tf_op jit(solution)/shard_map/dynamic_slice | solution.py:275
  1.3 0.1 broadcast_in_dim.8
  1.4 0.1 broadcast_in_dim.9.mask_ref
  1.5 0.7 %copy.8.positive_ref = s32[16,1]{1,0:T(8,128)S(1)} copy(s32[16,1]{0,1:T(1,128)} %bitcast.12) | data formatting | bytes 128 | tf_op jit(solution)/shard_map/broadcast_in_dim | solution.py:307
  2.2 0.0 copy-start
  2.2 0.9 %copy-done = bf16[16,32,128]{2,1,0:T(8,128)(2,1)S(1)} copy-done((bf16[16,32,128]{2,1,0:T(8,128)(2,1)S(1)}, bf16[16,32,128]{2,1,0:T(8,128)(2,1)}, u32[]{:S(2)}) %copy-start) | copy-done | bytes 131096
  3.1 0.0 copy-start.2
  3.1 0.9 %copy-done.2 = bf16[16,32,128]{2,1,0:T(8,128)(2,1)S(1)} copy-done((bf16[16,32,128]{2,1,0:T(8,128)(2,1)S(1)}, bf16[16,32,128]{2,1,0:T(8,128)(2,1)}, u32[]{:S(2)}) %copy-start.2) | copy-done | bytes 131096
  4.0 27.9 %gather_tokens.1 = (bf16[8192,128]{1,0:T(8,128)(2,1)S(1)}, bf16[8192,128]{1,0:T(8,128)(2,1)S(1)}) custom-call(bf16[512,128]{1,0:T(8,128)(2,1)S(1)} %bitcast.7, bf16[512,128]{1,0:T(8,128)(2,1)S(1)} %bitcast.9), custom_call_target="tpu_custom_call" | custom-call | tf_op jit(solution)/shard_map/gather_tokens/pallas_call | solution.py:141
  31.9 0.0 copy-start.4
  31.9 0.7 %copy-done.4 = s32[16,16]{1,0:T(8,128)S(1)} copy-done((s32[16,16]{1,0:T(8,128)S(1)}, s32[16,16]{1,0:T(8,128)}, u32[]{:S(2)}) %copy-start.4) | copy-done | bytes 1048
  32.6 0.0 copy-start.1
  32.6 0.0 copy-start.3
  32.6 5.1 %scores.1.refs_0_ = f32[16,256]{1,0:T(8,128)S(1)} custom-call(s32[16,16]{1,0:T(8,128)S(1)} %copy-done.4, bf16[512,128]{1,0:T(8,128)(2,1)S(1)} %bitcast.10, bf16[8192,128]{1,0:T(8,128)(2,1)S(1)} %get-tuple-element.9.clauses_ref, s32[1,256]{1,0:T(1,128)S(1)} %broadcast_in_dim.9.mask_ref), custom_call_target="tpu_custom_call" | custom-call | flops 2000000000 | bytes 4000000 | tf_op jit(solution)/shard_map/scores/pallas_call | solution.py:279
  37.7 14.5 %gather_scores.1.scores_ref = f32[256,256]{1,0:T(8,128)S(1)} custom-call(f32[16,256]{1,0:T(8,128)S(1)} %scores.1.refs_0_), custom_call_target="tpu_custom_call" | custom-call | tf_op jit(solution)/shard_map/gather_scores/pallas_call | solution.py:141
  52.2 0.0 copy-done.1
  52.2 0.0 copy-done.3
  52.2 12.9 %grads.1 = (f32[16,1]{1,0:T(8,128)S(1)}, f32[512,128]{1,0:T(8,128)}, f32[512,128]{1,0:T(8,128)}) custom-call(s32[16,16]{1,0:T(8,128)S(1)} %copy-done.4, bf16[8192,128]{1,0:T(8,128)(2,1)S(1)} %get-tuple-element.8.queries_ref, bf16[8192,128]{1,0:T(8,128)(2,1)S(1)} %get-tuple-element.9.clauses_ref, bf16[512,128]{1,0:T(8,128)(2,1)S(1)} %bitcast.11, ...), custom_call_target="tpu_custom_call" | custom-call | tf_op jit(solution)/shard_map/grads/pallas_call | solution.py:290
  65.1 0.6 reduce
Async XLA Ops:
  2.2 0.9 %copy-start = (bf16[16,32,128]{2,1,0:T(8,128)(2,1)S(1)}, bf16[16,32,128]{2,1,0:T(8,128)(2,1)}, u32[]{:S(2)}) copy-start(bf16[16,32,128]{2,1,0:T(8,128)(2,1)} %param.5) | copy-start | bytes 393220
  3.1 0.9 %copy-start.2 = (bf16[16,32,128]{2,1,0:T(8,128)(2,1)S(1)}, bf16[16,32,128]{2,1,0:T(8,128)(2,1)}, u32[]{:S(2)}) copy-start(bf16[16,32,128]{2,1,0:T(8,128)(2,1)} %param.4) | copy-start | bytes 393220
  31.9 0.7 %copy-start.4 = (s32[16,16]{1,0:T(8,128)S(1)}, s32[16,16]{1,0:T(8,128)}, u32[]{:S(2)}) copy-start(s32[16,16]{1,0:T(8,128)} %pattern_ref.3) | copy-start | bytes 3076
  32.6 19.6 %copy-start.1 = (bf16[16,32,128]{2,1,0:T(8,128)(2,1)S(1)}, bf16[16,32,128]{2,1,0:T(8,128)(2,1)}, u32[]{:S(2)}) copy-start(bf16[16,32,128]{2,1,0:T(8,128)(2,1)} %param.5) | copy-start | bytes 393220
  32.6 19.6 %copy-start.3 = (bf16[16,32,128]{2,1,0:T(8,128)(2,1)S(1)}, bf16[16,32,128]{2,1,0:T(8,128)(2,1)}, u32[]{:S(2)}) copy-start(bf16[16,32,128]{2,1,0:T(8,128)(2,1)} %param.4) | copy-start | bytes 393220
